TPU v7x, 32 devices: a whole 2x2x4 slice. The times are simulated.
32 devices in a mesh: grp: 4 (over y, x), tp: 8 (over z, core).
Axes of the slice: x: 2, y: 2, z: 4, core: 2. Of those that a mesh axis runs over, the one named last changes fastest.
Arguments:
- layer_input: bfloat16 [8192, 2048], P('grp'), may hold values from -6 to 6
- out_cotangent: bfloat16 [8192, 2048], P('grp'), may hold values from -6 to 6
- seq_group: int32 [6], replicated, may hold values from 0 to 3, as said below
- seq_len: int32 [6], replicated, may hold values from 512 to 2048, as said below
- w_qkv: float32 [2048, 6144], P('grp', 'tp'), may hold values from -0.1875 to 0.1875
- b_qv: float32 [4096], replicated, may hold values from -3 to 3
- w_out: float32 [2048, 2048], P('grp', 'tp'), may hold values from -0.75 to 0.75
- b_out: float32 [2048], replicated, may hold values from -2 to 2
- w_up: float32 [2048, 8192], P('grp', 'tp'), may hold values from -0.125 to 0.125
- b_up: float32 [8192], replicated, may hold values from -3 to 3
- w_down: float32 [2048, 8192], P('grp', 'tp'), may hold values from -0.0625 to 0.0625
- b_down: float32 [2048], replicated, may hold values from -2 to 2
- first_norm_gain: float32 [2048], replicated, may hold values from 0.1 to 1.9
- first_norm_bias: float32 [2048], replicated, may hold values from -2 to 2
- second_norm_gain: float32 [2048], replicated, may hold values from 0.1 to 1.9
- second_norm_bias: float32 [2048], replicated, may hold values from -2 to 2
Outputs:
- layer_output: bfloat16 [8192, 2048], P(('grp', 'tp'))
- grad_x: float32 [8192, 2048], P(('grp', 'tp'))
- grad_w_qkv: float32 [2048, 6144], P('grp', 'tp')
- grad_b_qv: float32 [4096], replicated
- grad_w_out: float32 [2048, 2048], P('grp', 'tp')
- grad_b_out: float32 [2048], replicated
- grad_w_up: float32 [2048, 8192], P('grp', 'tp')
- grad_b_up: float32 [8192], replicated
- grad_w_down: float32 [2048, 8192], P('grp', 'tp')
- grad_b_down: float32 [2048], replicated
- grad_ln1_gain: float32 [2048], replicated
- grad_ln1_bias: float32 [2048], replicated
- grad_ln2_gain: float32 [2048], replicated
- grad_ln2_bias: float32 [2048], replicated
Inputs may be any that keep to these rules, and one draw needn't show every extreme that they name: `seq_group`: each group's sequences total at most 2048 tokens, and in every draw some group holds exactly 2048; every group holds at least one sequence. `seq_len`: each sequence has 2048 or 512 tokens.
All inputs are finite; a program needn't handle non-finite values.
Results may differ from a plain program's by a relative error of at most 0.023.
Values may be sent and summed in bfloat16 or wider, within the bound.
A program may use at most 320 MiB of HBM per device.

v0:
```python
import jax
import jax.numpy as jnp
from jax import lax
from jax.sharding import PartitionSpec as P

HD = 128


def layer_normalize(rows, gain, bias):
    mean_row = jnp.mean(rows, -1, keepdims=True)
    centred = rows - mean_row
    inverse = lax.rsqrt(jnp.mean(centred * centred, -1, keepdims=True) + 1e-05)
    normed = centred * inverse
    return (normed * gain + bias, normed, inverse)


def norm_backward_pass(grad_norm, normed, inverse, gain):
    scaled = grad_norm * gain
    inner = jnp.mean(scaled, -1, keepdims=True) + normed * jnp.mean(
        scaled * normed, -1, keepdims=True
    )
    return inverse * (scaled - inner)


def contract(left, right, left_dim, right_dim):
    return lax.dot_general(
        left, right, (((left_dim,), (right_dim,)), ((), ())), preferred_element_type=jnp.float32
    )


def activate(values_in):
    return jax.nn.gelu(values_in, approximate=True)


def on_device(
    layer_input,
    out_cotangent,
    seq_group,
    seq_len,
    w_qkv,
    b_qv,
    w_out,
    b_out,
    w_up,
    b_up,
    w_down,
    b_down,
    first_norm_gain,
    first_norm_bias,
    second_norm_gain,
    second_norm_bias,
):
    w_attn, w_proj, w_expand, w_reduce = (
        lax.all_gather(w_qkv.astype(jnp.bfloat16), "grp", axis=0, tiled=True),
        lax.all_gather(w_out.astype(jnp.bfloat16), "grp", axis=0, tiled=True),
        lax.all_gather(w_up.astype(jnp.bfloat16), "grp", axis=0, tiled=True),
        lax.all_gather(w_down.astype(jnp.bfloat16), "grp", axis=0, tiled=True),
    )
    tp_rank = lax.axis_index("tp")
    tp_count = lax.axis_size("tp")
    group_rank = lax.axis_index("grp")
    length = layer_input.shape[0]
    shared_row_block = length // tp_count
    local_row_start = tp_rank * shared_row_block
    heads_here = w_proj.shape[1] // HD
    hidden_here = w_expand.shape[1]
    seq_count = seq_group.shape[0]
    in_group = seq_group == group_rank
    lengths = jnp.where(in_group, seq_len, 0)
    seq_order = jnp.arange(seq_count, dtype=jnp.int32)
    earlier = seq_order[:, None] > seq_order[None, :]
    offsets = jnp.sum(jnp.where(earlier, lengths[None, :], 0), 1)
    places = jnp.arange(length, dtype=jnp.int32)
    inside = (
        in_group[None, :]
        & (places[:, None] >= offsets[None, :])
        & (places[:, None] < (offsets + lengths)[None, :])
    )
    segment = jnp.sum(jnp.where(inside, seq_order[None, :] + 1, 0), 1) - 1
    live_rows = (segment >= 0).astype(jnp.float32)[:, None]
    input_row_block = layer_input.astype(jnp.float32)
    first_normalized, first_standardized, first_inverse_deviation = layer_normalize(
        input_row_block, first_norm_gain, first_norm_bias
    )
    normed_oneb = first_normalized.astype(jnp.bfloat16)
    head_bias = lax.dynamic_slice_in_dim(
        b_qv.reshape(-1, 2, HD), tp_rank * heads_here, heads_here, 0
    )
    bias_three = jnp.stack(
        [head_bias[:, 0], jnp.zeros_like(head_bias[:, 0]), head_bias[:, 1]], 1
    ).reshape(-1)
    projected = (
        jnp.dot(normed_oneb, w_attn, preferred_element_type=jnp.float32) + bias_three
    ).astype(jnp.bfloat16)
    projected = projected.reshape(length, heads_here, 3, HD)
    query = projected[:, :, 0]
    keys = projected[:, :, 1]
    values = projected[:, :, 2]
    block_rows = min(512, length)
    blocks = length // block_rows
    score_scale = HD ** (-0.5)
    columns = jnp.arange(length, dtype=jnp.int32)

    def scores_for(block_index):
        first_row = block_index * block_rows
        query_block = lax.dynamic_slice_in_dim(query, first_row, block_rows, 0)
        dotted = (
            jnp.einsum("qhe,khe->hqk", query_block, keys, preferred_element_type=jnp.float32)
            * score_scale
        )
        segment_block = lax.dynamic_slice_in_dim(segment, first_row, block_rows, 0)
        row_places = first_row + jnp.arange(block_rows, dtype=jnp.int32)
        allowed = (segment_block[:, None] == segment[None, :]) & (
            columns[None, :] <= row_places[:, None]
        )
        return (jnp.where(allowed[None], dotted, -1e30), query_block)

    def attend(block_index):
        masked, unused = scores_for(block_index)
        highest_score = jnp.max(masked, -1, keepdims=True)
        powers = jnp.exp(masked - highest_score)
        summed = jnp.sum(powers, -1, keepdims=True)
        chances = (powers / summed).astype(jnp.bfloat16)
        context = jnp.einsum(
            "hqk,khe->qhe", chances, values, preferred_element_type=jnp.float32
        ).astype(jnp.bfloat16)
        return (context, highest_score[..., 0] + jnp.log(summed[..., 0]))

    contexts, log_totals = lax.map(attend, jnp.arange(blocks))
    context_all = contexts.reshape(length, heads_here * HD)
    attn_total = lax.psum(contract(context_all, w_proj, 1, 1).astype(jnp.bfloat16), "tp").astype(
        jnp.float32
    )
    hidden_input = input_row_block + attn_total + b_out
    second_normalized, second_standardized, second_inverse_deviation = layer_normalize(
        hidden_input, second_norm_gain, second_norm_bias
    )
    normed_twob = second_normalized.astype(jnp.bfloat16)
    up_bias = lax.dynamic_slice_in_dim(b_up, tp_rank * hidden_here, hidden_here, 0)
    before = jnp.dot(normed_twob, w_expand, preferred_element_type=jnp.float32) + up_bias
    active = activate(before).astype(jnp.bfloat16)
    live_share = lax.dynamic_slice_in_dim(live_rows, local_row_start, shared_row_block, 0)
    mlp_total = lax.psum(contract(active, w_reduce, 1, 1).astype(jnp.bfloat16), "tp").astype(
        jnp.float32
    )
    out_share = (
        lax.dynamic_slice_in_dim(hidden_input, local_row_start, shared_row_block, 0)
        + lax.dynamic_slice_in_dim(mlp_total, local_row_start, shared_row_block, 0)
        + b_down
    )
    result = (live_share * out_share).astype(jnp.bfloat16)
    output_gradient = out_cotangent.astype(jnp.float32) * live_rows
    grad_outb = output_gradient.astype(jnp.bfloat16)
    grad_share = lax.dynamic_slice_in_dim(output_gradient, local_row_start, shared_row_block, 0)
    grad_reduce = contract(grad_outb, active, 0, 0)
    grad_active = jnp.dot(grad_outb, w_reduce, preferred_element_type=jnp.float32)
    unused, gelu_back = jax.vjp(activate, before)
    grad_beforeb = gelu_back(grad_active)[0].astype(jnp.bfloat16)
    grad_expand = contract(normed_twob, grad_beforeb, 0, 0)
    up_bias_part = jnp.sum(grad_beforeb.astype(jnp.float32), 0)
    second_norm_gradient = lax.psum(
        contract(grad_beforeb, w_expand, 1, 1).astype(jnp.bfloat16), "tp"
    ).astype(jnp.float32)
    hidden_gradient = output_gradient + norm_backward_pass(
        second_norm_gradient, second_standardized, second_inverse_deviation, second_norm_gain
    )
    grad_resb = hidden_gradient.astype(jnp.bfloat16)
    residual_share_gradient = lax.dynamic_slice_in_dim(
        hidden_gradient, local_row_start, shared_row_block, 0
    )
    second_norm_shared = lax.dynamic_slice_in_dim(
        second_norm_gradient, local_row_start, shared_row_block, 0
    )
    gain_two_grad = jnp.sum(
        second_norm_shared
        * lax.dynamic_slice_in_dim(second_standardized, local_row_start, shared_row_block, 0),
        0,
    )
    bias_two_grad = jnp.sum(second_norm_shared, 0)
    bias_out_grad = jnp.sum(residual_share_gradient, 0)
    down_bias_grad = jnp.sum(grad_share, 0)
    grad_proj = contract(grad_resb, context_all, 0, 0)
    grad_context = (
        jnp.dot(grad_resb, w_proj, preferred_element_type=jnp.float32)
        .astype(jnp.bfloat16)
        .reshape(length, heads_here, HD)
    )

    def attend_back(running, block_index):
        grad_keys, grad_values = running
        masked, query_block = scores_for(block_index)
        chances = jnp.exp(masked - log_totals[block_index][..., None])
        grad_block = lax.dynamic_slice_in_dim(grad_context, block_index * block_rows, block_rows, 0)
        grad_values = grad_values + jnp.einsum(
            "hqk,qhe->khe",
            chances.astype(jnp.bfloat16),
            grad_block,
            preferred_element_type=jnp.float32,
        )
        grad_chances = jnp.einsum(
            "qhe,khe->hqk", grad_block, values, preferred_element_type=jnp.float32
        )
        grad_scores = (
            chances * (grad_chances - jnp.sum(chances * grad_chances, -1, keepdims=True))
        ).astype(jnp.bfloat16)
        grad_query = (
            jnp.einsum("hqk,khe->qhe", grad_scores, keys, preferred_element_type=jnp.float32)
            * score_scale
        )
        grad_keys = (
            grad_keys
            + jnp.einsum(
                "hqk,qhe->khe", grad_scores, query_block, preferred_element_type=jnp.float32
            )
            * score_scale
        )
        return ((grad_keys, grad_values), grad_query)

    zeros_heads = jnp.zeros((length, heads_here, HD), jnp.float32)
    (grad_keys, grad_values), grad_queries = lax.scan(
        attend_back, (zeros_heads, zeros_heads), jnp.arange(blocks)
    )
    grad_queries = grad_queries.reshape(length, heads_here, HD)
    grad_projected = (
        jnp.stack([grad_queries, grad_keys, grad_values], 2)
        .astype(jnp.bfloat16)
        .reshape(length, heads_here * 3 * HD)
    )
    grad_attn = contract(normed_oneb, grad_projected, 0, 0)
    projected_sums = jnp.sum(grad_projected.astype(jnp.float32), 0).reshape(heads_here, 3, HD)
    query_value = jnp.stack([projected_sums[:, 0], projected_sums[:, 2]], 1)
    query_value_full = lax.dynamic_update_slice_in_dim(
        jnp.zeros((b_qv.shape[0] // (2 * HD), 2, HD), jnp.float32),
        query_value,
        tp_rank * heads_here,
        0,
    ).reshape(-1)
    up_bias_full = lax.dynamic_update_slice_in_dim(
        jnp.zeros(b_up.shape, jnp.float32), up_bias_part, tp_rank * hidden_here, 0
    )
    first_norm_gradient = lax.dynamic_slice_in_dim(
        lax.psum(contract(grad_projected, w_attn, 1, 1).astype(jnp.bfloat16), "tp").astype(
            jnp.float32
        ),
        local_row_start,
        shared_row_block,
        0,
    )
    shared_standardized = lax.dynamic_slice_in_dim(
        first_standardized, local_row_start, shared_row_block, 0
    )
    shared_inverse_deviation = lax.dynamic_slice_in_dim(
        first_inverse_deviation, local_row_start, shared_row_block, 0
    )
    input_gradient = residual_share_gradient + norm_backward_pass(
        first_norm_gradient, shared_standardized, shared_inverse_deviation, first_norm_gain
    )
    first_gain_gradient = jnp.sum(first_norm_gradient * shared_standardized, 0)
    bias_one_grad = jnp.sum(first_norm_gradient, 0)
    grads_attn, grads_proj, grads_expand, grads_reduce = (
        lax.psum_scatter(
            grad_attn.astype(jnp.bfloat16), "grp", scatter_dimension=0, tiled=True
        ).astype(jnp.float32),
        lax.psum_scatter(
            grad_proj.astype(jnp.bfloat16), "grp", scatter_dimension=0, tiled=True
        ).astype(jnp.float32),
        lax.psum_scatter(
            grad_expand.astype(jnp.bfloat16), "grp", scatter_dimension=0, tiled=True
        ).astype(jnp.float32),
        lax.psum_scatter(
            grad_reduce.astype(jnp.bfloat16), "grp", scatter_dimension=0, tiled=True
        ).astype(jnp.float32),
    )
    small_grads = lax.psum(
        (
            query_value_full,
            bias_out_grad,
            up_bias_full,
            down_bias_grad,
            first_gain_gradient,
            bias_one_grad,
            gain_two_grad,
            bias_two_grad,
        ),
        ("grp", "tp"),
    )
    return (
        result,
        input_gradient,
        grads_attn,
        small_grads[0],
        grads_proj,
        small_grads[1],
        grads_expand,
        small_grads[2],
        grads_reduce,
        small_grads[3],
        small_grads[4],
        small_grads[5],
        small_grads[6],
        small_grads[7],
    )


def solution(mesh):
    in_specs = (
        P("grp", None),
        P("grp", None),
        P(),
        P(),
        P("grp", "tp"),
        P(),
        P("grp", "tp"),
        P(),
        P("grp", "tp"),
        P(),
        P("grp", "tp"),
        P(),
        P(),
        P(),
        P(),
        P(),
    )
    out_specs = (
        P(("grp", "tp"), None),
        P(("grp", "tp"), None),
        P("grp", "tp"),
        P(),
        P("grp", "tp"),
        P(),
        P("grp", "tp"),
        P(),
        P("grp", "tp"),
        P(),
        P(),
        P(),
        P(),
        P(),
    )
    return jax.shard_map(
        on_device, mesh=mesh, in_specs=in_specs, out_specs=out_specs, check_vma=False
    )
```

profile of v0, /device:TPU:8, one launch (start us, length us, event | category | flops | bytes accessed | tf_op | source)
XLA Modules:
  0.0 1345.7 jit_solution(15598600205464487332)
XLA Ops:
  13.4 4.7 convert_reduce_fusion
  21.6 34.0 %all-gather.5.cloned.1.call-done = bf16[2048,768]{1,0:T(8,128)(2,1)} async-done(((bf16[512,768]{1,0:T(8,128)(2,1)}), bf16[2048,768]{1,0:T(8,128)(2,1)}) %all-gather.5.cloned.1.call-update) | async-done | bytes 3145744 | tf_op jit(solution)/shard_map/all_gather | solution.py:54
  55.6 11.5 add_convert_fusion.2
  71.4 46.1 %while.28 = (s32[]{:T(128)}, bf16[4,512,2,128]{3,2,1,0:T(2,128)(2,1)}, f32[4,2,512]{2,1,0:T(2,128)}, s32[4]{0:T(128)S(1)}, s32[2048]{0:T(1024)S(1)}, /*index=5*/...) while((s32[]{:T(128)}, ...), condition=%wide.region_7.8_spmd.clone, body=%wide.region_4.7_spmd.clone.sunk | while | flops 1102183936 | bytes 32557260 | solution.py:129
  75.9 2.5 fusion.135
  78.4 2.9 fusion.136
  87.4 2.5 fusion.135
  89.9 2.9 fusion.136
  98.9 2.5 fusion.135
  101.4 2.9 fusion.136
  110.4 2.5 fusion.135
  112.9 2.9 fusion.136
  117.5 8.2 convolution_convert_fusion.3
  125.9 2.7 convert_element_type.139
  128.7 2.7 convert_element_type.141
  132.2 169.3 %all-reduce.7.cloned.1.call-done = bf16[2048,2048]{1,0:T(8,128)(2,1)} async-done(((bf16[2048,2048]{1,0:T(8,128)(2,1)}), bf16[2048,2048]{1,0:T(8,128)(2,1)}) %all-reduce.7.cloned.1.call-update) | async-done | bytes 8388624 | tf_op jit(solution)/shard_map/psum | solution.py:131
  301.5 17.6 %fusion.88 = (f32[2048]{0:T(1024)S(1)}, f32[2048,2048]{1,0:T(8,128)}, f32[2048,2048]{1,0:T(8,128)}) fusion(f32[2048]{0:T(1024)S(1)} %copy-done.25, bf16[2048,2048]{1,0:T(8,128)(2,1)} %all-reduce.7.cloned.1.call-done, bf16[2048,2048]{1,0:T(8,128)(2,1)} %param.20, f32[2048]{0:T(1024)S(1)} %add_rsqrt_fusion.1, f32[2048]{0:T(1024)S(1)} %broadcast_multiply_fusion.3), kind=kLoop, calls=%fused_computation.141 | loop fusion | flops 29358080 | bytes 50364416 | tf_op jit(solution)/shard_map/reduce_sum | solution.py:10
  319.1 7.6 multiply_reduce_fusion.2
  326.7 11.8 subtract_multiply_fusion
  338.5 18.2 %all-gather.9.cloned.1.call-done = bf16[2048,1024]{1,0:T(8,128)(2,1)} async-done(((bf16[512,1024]{1,0:T(8,128)(2,1)}), bf16[2048,1024]{1,0:T(8,128)(2,1)}) %all-gather.9.cloned.1.call-update) | async-done | bytes 4194320 | tf_op jit(solution)/shard_map/all_gather | solution.py:56
  356.7 15.5 %fusion.75 = f32[2048,1024]{1,0:T(8,128)} fusion(bf16[2048,1024]{1,0:T(8,128)(2,1)} %all-gather.9.cloned.1.call-done, f32[2048,2048]{1,0:T(8,128)} %subtract_multiply_fusion, f32[2048]{0:T(1024)S(1)} %copy-done.31, f32[2048]{0:T(1024)S(1)} %copy-done.21), kind=kOutput, calls=%fused_computation.102 | convolution fusion | flops 8602517504 | bytes 29376512 | tf_op jit(solution)/shard_map/dot_general | solution.py:140
  372.2 39.5 %all-gather.11.cloned.1.call-done = bf16[2048,1024]{1,0:T(8,128)(2,1)} async-done(((bf16[512,1024]{1,0:T(8,128)(2,1)}), bf16[2048,1024]{1,0:T(8,128)(2,1)}) %all-gather.11.cloned.1.call-update) | async-done | bytes 4194320 | tf_op jit(solution)/shard_map/all_gather | solution.py:57
  411.7 19.5 %convert_reduce_fusion.1 = (f32[1024]{0:T(1024)}, bf16[2048,1024]{1,0:T(8,128)(2,1)S(1)}) fusion(f32[2048,1024]{1,0:T(8,128)} %fusion.75, f32[1024]{0:T(1024)S(1)} %dynamic_slice.59, bf16[2048,1024]{1,0:T(8,128)(2,1)} %all-gather.11.cloned.1.call-done, f32[2048]{0:T(1024)S(1)} %compare_convert_fusion, bf16[2048,2048]{1,0:T(8,128)(2,1)} %param.21), kind=kOutput, calls=%fused_computation.74 | convolution fusion | flops 8650750976 | bytes 25182208 | tf_op jit(solution)/shard_map/dot_general | solution.py:156
  433.2 10.9 convolution_convert_fusion.1
  444.1 175.7 %all-reduce.9.cloned.1.call-done = bf16[2048,2048]{1,0:T(8,128)(2,1)} async-done(((bf16[2048,2048]{1,0:T(8,128)(2,1)}), bf16[2048,2048]{1,0:T(8,128)(2,1)}) %all-reduce.9.cloned.1.call-update) | async-done | bytes 8388624 | tf_op jit(solution)/shard_map/psum | solution.py:161
  619.8 10.5 multiply_reduce_fusion.3
  630.3 19.1 %convert_multiply_fusion = (f32[2048,2048]{1,0:T(8,128)}, f32[2048,2048]{1,0:T(8,128)S(1)}) fusion(bf16[2048,2048]{1,0:T(8,128)(2,1)} %param.21, f32[2048]{0:T(1024)S(1)} %compare_convert_fusion, f32[2048]{0:T(1024)S(1)} %broadcast_multiply_fusion, f32[2048]{0:T(1024)S(1)} %broadcast_multiply_fusion.1, f32[2048]{0:T(1024)S(1)} %copy-done.21, ...), kind=kLoop, calls=%fused_computation.59 | loop fusion | flops 46137344 | bytes 67158016 | tf_op jit(solution)/shard_map/mul | solution.py:152
  649.4 5.7 copy-done
  655.1 3.6 fusion.70
  658.8 16.8 %fusion.61 = bf16[2048,1024]{1,0:T(8,128)(2,1)} fusion(bf16[2048,2048]{1,0:T(8,128)(2,1)} %param.21, f32[2048]{0:T(1024)S(1)} %compare_convert_fusion, f32[2048,1024]{1,0:T(8,128)} %fusion.75, f32[1024]{0:T(1024)S(1)} %dynamic_slice.59), kind=kOutput, calls=%fused_computation.91 | convolution fusion | flops 8625586176 | bytes 20983808 | tf_op jit(solution)/shard_map/dot_general | solution.py:26
  675.7 15.3 %convolution_convert_fusion.4 = bf16[2048,1024]{1,0:T(8,128)(2,1)} fusion(bf16[2048,1024]{1,0:T(8,128)(2,1)} %copy-done.34, f32[2048,2048]{1,0:T(8,128)} %subtract_multiply_fusion, f32[2048]{0:T(1024)S(1)} %copy-done.31, f32[2048]{0:T(1024)S(1)} %copy-done.21), kind=kOutput, calls=%fused_computation.92 | convolution fusion | flops 8604614656 | bytes 25182208 | tf_op jit(solution)/shard_map/dot_general | solution.py:26
  691.1 9.8 fusion.67
  700.9 89.8 %while.29 = (s32[]{:T(128)}, f32[2048,2,128]{0,2,1:T(8,128)S(1)}, f32[2048,2,128]{0,2,1:T(8,128)}, bf16[4,512,2,128]{3,1,0,2:T(8,128)(2,1)}, s32[4]{0:T(128)S(1)...) while((s32[]{:T(128)}, f32[2048,2,128]{0,2,1:T(8,128)S(1)}, ...), condition=%wide.region_17.18_spmd.clone, body=%wide.region_15.17_spmd.clone.sunk | while | flops 2721709568 | bytes 97040784 | solution.py:220
  708.6 3.7 fusion.149
  712.3 3.8 multiply_reduce_fusion.6
  716.2 2.6 multiply_convert_fusion.6
  720.1 2.4 fusion.148
  730.1 5.0 fusion.149
  735.1 3.9 multiply_reduce_fusion.6
  739.0 2.6 multiply_convert_fusion.6
  742.9 2.4 fusion.148
  752.8 5.0 fusion.149
  757.8 3.8 multiply_reduce_fusion.6
  761.7 2.6 multiply_convert_fusion.6
  765.6 2.4 fusion.148
  775.5 5.0 fusion.149
  780.5 3.9 multiply_reduce_fusion.6
  784.4 2.6 multiply_convert_fusion.6
  788.3 2.4 fusion.148
  792.1 2.7 copy.79
  797.2 2.9 copy.80
  800.1 13.1 convolution_convert_fusion.5
  813.2 17.8 %convolution_convert_fusion.2 = bf16[2048,2048]{1,0:T(8,128)(2,1)} fusion(bf16[2048,1024]{1,0:T(8,128)(2,1)} %all-gather.11.cloned.1.call-done, f32[2048,1024]{1,0:T(8,128)} %fusion.75, f32[1024]{0:T(1024)S(1)} %copy-done.28), kind=kOutput, calls=%fused_computation.78 | convolution fusion | flops 8615100416 | bytes 20975616 | tf_op jit(solution)/shard_map/dot_general | solution.py:26
  831.1 9.2 convolution_convert_fusion
  841.7 11.3 convert_element_type.149
  855.3 3.2 dynamic-slice_reduce_fusion.1
  860.4 2.8 convert_element_type.165
  863.2 2.8 convert_element_type.162
  866.0 2.5 convert_element_type.157
  868.6 325.1 %all-reduce.13.cloned.1.call-done = (bf16[2048,2048]{1,0:T(8,128)(2,1)}, bf16[2048,2048]{1,0:T(8,128)(2,1)}) async-done(((bf16[2048,2048]{1,0:T(8,128)(2,1)}, bf16[2048,2048]{1,0:T(8,128)(2,1)}), (bf16[2048,2048]{1,0:T(8,128)(2,1)}, bf16[2048,2048]{1,0:T(8,128)(2,1)})) %all-reduce.13.cloned.1.call-update) | async-done | bytes 16777232 | tf_op jit(solution)/shard_map/psum | solution.py:143
  1193.6 3.2 fusion.79
  1196.9 5.2 dynamic-slice_reduce_fusion.2
  1202.1 3.2 multiply_convert_fusion.2
  1205.3 122.7 %all-reduce.11.cloned.1.call-done = (f32[4096]{0:T(1024)}, f32[2048]{0:T(1024)}, f32[8192]{0:T(1024)}, f32[2048]{0:T(1024)}, f32[2048]{0:T(1024)}, /*index=5*/f32[2048]{0:T(1024)}, f32[2048]{0:T(1024)}, f32[2048]{0:T(1024)}) async-done(((f32[4096]{0:T(1024)}, f32[2048]{0:T(1024)}, f32[8192]{0:T(1024)}, f32[2048]{0:T(1024)}, f32[2048]{0:T(1024)}, /*index=5*/f32[2048]{0:T(1024)}, f32[2048]{0:T(1024)}, ...) | async-done | bytes 98320 | tf_op jit(solution)/shard_map/psum | solution.py:274
  (231 shorter events, 83.4 us)
Async XLA Ops:
  7.2 48.4 %all-gather.5.cloned.1.call-start = ((), (), s32[]{:S(2)}) async-start(), calls=%async_computation.4 | async-start | bytes 3932160 | tf_op jit(solution)/shard_map/all_gather | solution.py:54
  9.6 107.9 %all-gather.7.cloned.1.call-start = ((), (), s32[]{:S(2)}) async-start(), calls=%async_computation.5 | async-start | bytes 1310720 | tf_op jit(solution)/shard_map/all_gather | solution.py:55
  11.5 290.1 %all-reduce.7.cloned.1.call-start = ((), (), s32[]{:S(2)}) async-start(), calls=%async_computation.6 | async-start | bytes 16777216 | tf_op jit(solution)/shard_map/psum | solution.py:131
  13.3 6.0 copy-start.3
  13.4 42.2 %copy-start.22 = (f32[2048]{0:T(1024)S(1)}, f32[2048]{0:T(1024)}, u32[]{:S(2)}) copy-start(f32[2048]{0:T(1024)} %param.32) | copy-start | bytes 24580
  13.4 42.2 %copy-start.32 = (f32[2048]{0:T(1024)S(1)}, f32[2048]{0:T(1024)}, u32[]{:S(2)}) copy-start(f32[2048]{0:T(1024)} %param.33) | copy-start | bytes 24580
  19.2 282.3 %copy-start.15 = (f32[2048]{0:T(1024)}, f32[2048]{0:T(1024)S(1)}, u32[]{:S(2)}) copy-start(f32[2048]{0:T(1024)S(1)} %broadcast_multiply_fusion.3) | copy-start | bytes 24580
  21.6 280.0 %copy-start.19 = (f32[2048]{0:T(1024)}, f32[2048]{0:T(1024)S(1)}, u32[]{:S(2)}) copy-start(f32[2048]{0:T(1024)S(1)} %add_rsqrt_fusion.1) | copy-start | bytes 24580
  117.5 8.3 copy-start.1
  117.5 8.3 copy-start.4
  117.5 8.3 copy-start.6
  117.5 8.3 copy-start.10
  125.8 175.8 %copy-start.25 = (f32[2048]{0:T(1024)S(1)}, f32[2048]{0:T(1024)}, u32[]{:S(2)}) copy-start(f32[2048]{0:T(1024)} %param.27) | copy-start | bytes 24580
  125.8 230.8 %all-gather.9.cloned.1.call-start = ((), (), s32[]{:S(2)}) async-start(), calls=%async_computation.7 | async-start | bytes 5242880 | tf_op jit(solution)/shard_map/all_gather | solution.py:56
  128.6 283.0 %all-gather.11.cloned.1.call-start = ((), (), s32[]{:S(2)}) async-start(), calls=%async_computation.8 | async-start | bytes 5242880 | tf_op jit(solution)/shard_map/all_gather | solution.py:57
  131.4 488.4 %all-reduce.9.cloned.1.call-start = ((), (), s32[]{:S(2)}) async-start(), calls=%async_computation.9 | async-start | bytes 16777216 | tf_op jit(solution)/shard_map/psum | solution.py:161
  131.5 527.3 %copy-start.18 = (f32[2048]{0:T(1024)}, f32[2048]{0:T(1024)S(1)}, u32[]{:S(2)}) copy-start(f32[2048]{0:T(1024)S(1)} %compare_convert_fusion) | copy-start | bytes 24580
  132.2 526.6 %copy-start.27 = (f32[1024]{0:T(1024)}, f32[1024]{0:T(1024)S(1)}, u32[]{:S(2)}) copy-start(f32[1024]{0:T(1024)S(1)} %dynamic_slice.59) | copy-start | bytes 12292
  326.7 30.0 %copy-start.21 = (f32[2048]{0:T(1024)S(1)}, f32[2048]{0:T(1024)}, u32[]{:S(2)}) copy-start(f32[2048]{0:T(1024)} %param.34) | copy-start | bytes 24580
  326.7 30.0 %copy-start.31 = (f32[2048]{0:T(1024)S(1)}, f32[2048]{0:T(1024)}, u32[]{:S(2)}) copy-start(f32[2048]{0:T(1024)} %param.35) | copy-start | bytes 24580
  411.7 21.5 %copy-start.29 = (bf16[2048,1024]{1,0:T(8,128)(2,1)S(1)}, bf16[2048,1024]{1,0:T(8,128)(2,1)}, u32[]{:S(2)}) copy-start(bf16[2048,1024]{1,0:T(8,128)(2,1)} %all-gather.9.cloned.1.call-done) | copy-start | bytes 12582916
  431.2 2.0 copy-start.34
  444.1 414.6 %reduce-scatter.7.cloned.1.call-start = ((), (), s32[]{:S(2)}) async-start(), calls=%async_computation.11 | async-start | bytes 1310720 | tf_op jit(solution)/shard_map/reduce_scatter | solution.py:264
  630.3 24.8 %copy-start.8 = (bf16[4,512,2,128]{3,2,1,0:T(2,128)(2,1)S(1)}, bf16[4,512,2,128]{3,2,1,0:T(2,128)(2,1)}, u32[]{:S(2)}) copy-start(bf16[4,512,2,128]{3,2,1,0:T(2,128)(2,1)} %get-tuple-element.126) | copy-start | bytes 3145732
  649.4 5.7 copy-start
  658.7 201.7 %reduce-scatter.11.cloned.1.call-start = ((), (), s32[]{:S(2)}) async-start(), calls=%async_computation.13 | async-start | bytes 5242880 | tf_op jit(solution)/shard_map/reduce_scatter | solution.py:270
  675.7 187.6 %reduce-scatter.9.cloned.1.call-start = ((), (), s32[]{:S(2)}) async-start(), calls=%async_computation.12 | async-start | bytes 5242880 | tf_op jit(solution)/shard_map/reduce_scatter | solution.py:267
  691.1 9.8 copy-start.2
  691.1 9.8 copy-start.11
  691.1 174.9 %reduce-scatter.5.cloned.1.call-start = ((), (), s32[]{:S(2)}) async-start(), calls=%async_computation.10 | async-start | bytes 3932160 | tf_op jit(solution)/shard_map/reduce_scatter | solution.py:261
  704.3 4.3 copy-start.7
  708.6 3.7 copy-start.5
  716.2 2.6 copy-start.12
  720.1 2.4 copy-start.13
  725.7 4.4 copy-start.7
  730.1 5.0 copy-start.5
  739.0 2.6 copy-start.12
  742.9 2.4 copy-start.13
  748.5 4.3 copy-start.7
  752.8 5.0 copy-start.5
  761.7 2.6 copy-start.12
  765.6 2.4 copy-start.13
  771.2 4.3 copy-start.7
  775.5 5.0 copy-start.5
  784.4 2.6 copy-start.12
  788.3 2.4 copy-start.13
  792.1 7.9 copy-start.16
  792.1 7.9 copy-start.20
  792.1 7.9 copy-start.23
  792.1 7.9 copy-start.33
  800.1 13.2 copy-start.28
  813.2 17.9 %copy-start.9 = (bf16[2048,2,3,128]{0,3,2,1:T(8,128)(2,1)S(1)}, bf16[2048,2,3,128]{0,3,2,1:T(8,128)(2,1)}, u32[]{:S(2)}) copy-start(bf16[2048,2,3,128]{0,3,2,1:T(8,128)(2,1)} %copy.80) | copy-start | bytes 9437188
  813.2 380.5 %all-reduce.13.cloned.1.call-start = ((), (), s32[]{:S(2)}) async-start(), calls=%async_computation.15 | async-start | bytes 33554432 | tf_op jit(solution)/shard_map/psum | solution.py:143
  813.2 17.8 %copy-start.30 = (bf16[2048,768]{1,0:T(8,128)(2,1)S(1)}, bf16[2048,768]{1,0:T(8,128)(2,1)}, u32[]{:S(2)}) copy-start(bf16[2048,768]{1,0:T(8,128)(2,1)} %all-gather.5.cloned.1.call-done) | copy-start | bytes 9437188
  840.2 0.9 copy-start.26
  840.2 487.7 %all-reduce.11.cloned.1.call-start = ((), (), s32[]{:S(2)}) async-start(), calls=%async_computation.14 | async-start | bytes 196608 | tf_op jit(solution)/shard_map/psum | solution.py:274
  841.7 11.3 copy-start.14
  858.6 343.5 %copy-start.17 = (f32[16,2,128]{2,1,0:T(2,128)}, f32[16,2,128]{2,1,0:T(2,128)S(1)}, u32[]{:S(2)}) copy-start(f32[16,2,128]{2,1,0:T(2,128)S(1)} %constant_dynamic-update-slice_fusion) | copy-start | bytes 49156
  863.2 338.9 %copy-start.24 = (f32[2048]{0:T(1024)S(1)}, f32[2048]{0:T(1024)}, u32[]{:S(2)}) copy-start(f32[2048]{0:T(1024)} %param.31) | copy-start | bytes 24580
Sparse Core Ops, SparseCore 0:
  10.4 45.1 all-gather.4
  58.0 26.6 all-gather.6
  125.9 175.5 all-reduce.6
  303.8 52.8 all-gather.8
  358.9 52.6 all-gather.10
  444.2 175.5 all-reduce.8
  658.8 27.8 reduce-scatter.6
  690.0 52.6 reduce-scatter.10
  745.7 52.6 reduce-scatter.8
  813.3 43.9 reduce-scatter.4
  860.1 333.5 all-reduce.12
  1202.2 125.6 all-reduce.10
where the time goes:
time: 1350 us
  waiting for transfers between devices  885 us (66%)
  matrix products  229 us (17%)
  other arithmetic  157 us (12%)
  local copies, waits for them, and re-layouts  45.9 us (3%)
  between operations  15.2 us (1%)
  loops' own time  14 us (1%)
    psum x1, waiting for transfers between devices, on_device(): lax.psum(contract(active, w_reduce, 1, 1).astype(jnp.bfloat16), 'tp')  325 us
    psum x1, waiting for transfers between devices, on_device(): lax.psum(contract(grad_beforeb, w_expand, 1, 1).astype(jnp.bfloat16), 'tp')  176 us
    psum x1, waiting for transfers between devices, on_device(): lax.psum(contract(context_all, w_proj, 1, 1).astype(jnp.bfloat16), 'tp')  169 us
    psum x1, waiting for transfers between devices, on_device(): lax.psum((query_value_full, bias_out_grad, up_bias_full, down_bias_grad,...  123 us
    dot_general x8, matrix products, contract(): lax.dot_general(left, right, (((left_dim,), (right_dim,)), ((), ())), pre...  94.9 us
    all_gather x1, waiting for transfers between devices, on_device(): lax.all_gather(w_down.astype(jnp.bfloat16), 'grp', axis=0, tiled=True)  39.5 us
    all_gather x1, waiting for transfers between devices, on_device(): lax.all_gather(w_qkv.astype(jnp.bfloat16), 'grp', axis=0, tiled=True)  34 us
  transfers between devices with their start and end apart: 12, of which 7 were waited for; matrix products, arithmetic and copies ran while one was open for 24% of the time, Pallas kernels for 0%

commit v1 on v0

--- a/solution.py
+++ b/solution.py
@@ -272,17 +272,20 @@
         ).astype(jnp.float32),
     )
     small_grads = lax.psum(
-        (
-            query_value_full,
-            bias_out_grad,
-            up_bias_full,
-            down_bias_grad,
-            first_gain_gradient,
-            bias_one_grad,
-            gain_two_grad,
-            bias_two_grad,
+        lax.psum(
+            (
+                query_value_full,
+                bias_out_grad,
+                up_bias_full,
+                down_bias_grad,
+                first_gain_gradient,
+                bias_one_grad,
+                gain_two_grad,
+                bias_two_grad,
+            ),
+            "tp",
         ),
-        ("grp", "tp"),
+        "grp",
     )
     return (
         result,

time: 1350 us -> 1430 us (1.059)
  waiting for transfers between devices: 885 us -> 953 us
    psum x1, waiting for transfers between devices: 123 us -> 55.9 us  [on_device(): lax.psum((query_value_full, bias_out_grad, up_bias_full, down_bias_grad,...]
    psum x1, waiting for transfers between devices: 325 us -> 260 us  [on_device(): lax.psum(contract(active, w_reduce, 1, 1).astype(jnp.bfloat16), 'tp')]
    reduce_scatter x1, waiting for transfers between devices: 0.01 us -> 54.2 us  [on_device(): lax.psum_scatter(grad_reduce.astype(jnp.bfloat16), 'grp', scatter_dimensi...]
    reduce_scatter x1, waiting for transfers between devices: 0.01 us -> 52.7 us  [on_device(): lax.psum_scatter(grad_expand.astype(jnp.bfloat16), 'grp', scatter_dimensi...]
    reduce_scatter x1, waiting for transfers between devices: 0.01 us -> 44.5 us  [on_device(): lax.psum_scatter(grad_attn.astype(jnp.bfloat16), 'grp', scatter_dimension...]
    psum x0 -> x1, waiting for transfers between devices: none -> 44.1 us  [on_device(): lax.psum(lax.psum((query_value_full, bias_out_grad, up_bias_full, down_bi...]
    reduce_scatter x1, waiting for transfers between devices: 0.02 us -> 22.7 us  [on_device(): lax.psum_scatter(grad_proj.astype(jnp.bfloat16), 'grp', scatter_dimension...]
    psum x1, waiting for transfers between devices: 176 us -> 158 us  [on_device(): lax.psum(contract(grad_beforeb, w_expand, 1, 1).astype(jnp.bfloat16), 'tp')]
  transfers between devices with their start and end apart: 12 -> 13, of which waited for: 7 -> 12; matrix products, arithmetic and copies ran while one was open for 24% -> 17% of each run, Pallas kernels for 0% -> 0%
where the time goes in v1:
time: 1430 us; the launch traced here: 1420 us
  waiting for transfers between devices  953 us (67%)
  matrix products  236 us (17%)
  other arithmetic  159 us (11%)
  local copies, waits for them, and re-layouts  40.8 us (3%)
  between operations  14.9 us (1%)
    psum x1, waiting for transfers between devices, on_device(): lax.psum(contract(active, w_reduce, 1, 1).astype(jnp.bfloat16), 'tp')  260 us
    psum x1, waiting for transfers between devices, on_device(): lax.psum(contract(context_all, w_proj, 1, 1).astype(jnp.bfloat16), 'tp')  169 us
    psum x1, waiting for transfers between devices, on_device(): lax.psum(contract(grad_beforeb, w_expand, 1, 1).astype(jnp.bfloat16), 'tp')  158 us
    dot_general x8, matrix products, contract(): lax.dot_general(left, right, (((left_dim,), (right_dim,)), ((), ())), pre...  103 us
    psum x1, waiting for transfers between devices, on_device(): lax.psum((query_value_full, bias_out_grad, up_bias_full, down_bias_grad,...  55.9 us
    reduce_scatter x1, waiting for transfers between devices, on_device(): lax.psum_scatter(grad_reduce.astype(jnp.bfloat16), 'grp', scatter_dimensi...  54.2 us
    reduce_scatter x1, waiting for transfers between devices, on_device(): lax.psum_scatter(grad_expand.astype(jnp.bfloat16), 'grp', scatter_dimensi...  52.7 us
    reduce_scatter x1, waiting for transfers between devices, on_device(): lax.psum_scatter(grad_attn.astype(jnp.bfloat16), 'grp', scatter_dimension...  44.5 us
  transfers between devices with their start and end apart: 13, of which 12 were waited for; matrix products, arithmetic and copies ran while one was open for 17% of the time, Pallas kernels for 0%

profile of v1, /device:TPU:8, one launch (start us, length us, event | category | flops | bytes accessed | tf_op | source)
XLA Modules:
  0.0 1418.4 jit_solution(1209002106334912166)
XLA Ops:
  13.4 4.7 convert_reduce_fusion
  21.6 34.0 %all-gather.5.cloned.1.call-done = bf16[2048,768]{1,0:T(8,128)(2,1)} async-done(((bf16[512,768]{1,0:T(8,128)(2,1)}), bf16[2048,768]{1,0:T(8,128)(2,1)}) %all-gather.5.cloned.1.call-update) | async-done | bytes 3145744 | tf_op jit(solution)/shard_map/all_gather | solution.py:54
  55.6 11.5 add_convert_fusion.2
  71.4 46.1 %while.28 = (s32[]{:T(128)}, bf16[4,512,2,128]{3,2,1,0:T(2,128)(2,1)}, f32[4,2,512]{2,1,0:T(2,128)}, s32[4]{0:T(128)S(1)}, s32[2048]{0:T(1024)S(1)}, /*index=5*/...) while((s32[]{:T(128)}, ...), condition=%wide.region_7.8_spmd.clone, body=%wide.region_4.7_spmd.clone.sunk | while | flops 1102183936 | bytes 32557260 | solution.py:129
  75.9 2.5 fusion.135
  78.4 2.9 fusion.136
  87.4 2.5 fusion.135
  89.9 2.9 fusion.136
  98.9 2.5 fusion.135
  101.4 2.9 fusion.136
  110.4 2.5 fusion.135
  112.9 2.9 fusion.136
  117.5 8.2 convolution_convert_fusion.3
  125.9 2.7 convert_element_type.139
  128.7 2.7 convert_element_type.141
  132.2 169.3 %all-reduce.9.cloned.1.call-done = bf16[2048,2048]{1,0:T(8,128)(2,1)} async-done(((bf16[2048,2048]{1,0:T(8,128)(2,1)}), bf16[2048,2048]{1,0:T(8,128)(2,1)}) %all-reduce.9.cloned.1.call-update) | async-done | bytes 8388624 | tf_op jit(solution)/shard_map/psum | solution.py:131
  301.5 17.6 %fusion.88 = (f32[2048]{0:T(1024)S(1)}, f32[2048,2048]{1,0:T(8,128)}, f32[2048,2048]{1,0:T(8,128)}) fusion(f32[2048]{0:T(1024)S(1)} %copy-done.28, bf16[2048,2048]{1,0:T(8,128)(2,1)} %all-reduce.9.cloned.1.call-done, bf16[2048,2048]{1,0:T(8,128)(2,1)} %param.20, f32[2048]{0:T(1024)S(1)} %add_rsqrt_fusion.1, f32[2048]{0:T(1024)S(1)} %broadcast_multiply_fusion.3), kind=kLoop, calls=%fused_computation.141 | loop fusion | flops 29358080 | bytes 50364416 | tf_op jit(solution)/shard_map/reduce_sum | solution.py:10
  319.1 7.6 multiply_reduce_fusion.2
  326.7 11.8 subtract_multiply_fusion
  338.5 18.2 %all-gather.9.cloned.1.call-done = bf16[2048,1024]{1,0:T(8,128)(2,1)} async-done(((bf16[512,1024]{1,0:T(8,128)(2,1)}), bf16[2048,1024]{1,0:T(8,128)(2,1)}) %all-gather.9.cloned.1.call-update) | async-done | bytes 4194320 | tf_op jit(solution)/shard_map/all_gather | solution.py:56
  356.7 15.5 %fusion.75 = f32[2048,1024]{1,0:T(8,128)} fusion(bf16[2048,1024]{1,0:T(8,128)(2,1)} %all-gather.9.cloned.1.call-done, f32[2048,2048]{1,0:T(8,128)} %subtract_multiply_fusion, f32[2048]{0:T(1024)S(1)} %copy-done.33, f32[2048]{0:T(1024)S(1)} %copy-done.23), kind=kOutput, calls=%fused_computation.102 | convolution fusion | flops 8602517504 | bytes 29376512 | tf_op jit(solution)/shard_map/dot_general | solution.py:140
  372.2 39.5 %all-gather.11.cloned.1.call-done = bf16[2048,1024]{1,0:T(8,128)(2,1)} async-done(((bf16[512,1024]{1,0:T(8,128)(2,1)}), bf16[2048,1024]{1,0:T(8,128)(2,1)}) %all-gather.11.cloned.1.call-update) | async-done | bytes 4194320 | tf_op jit(solution)/shard_map/all_gather | solution.py:57
  411.7 19.5 %convert_reduce_fusion.1 = (f32[1024]{0:T(1024)}, bf16[2048,1024]{1,0:T(8,128)(2,1)S(1)}) fusion(f32[2048,1024]{1,0:T(8,128)} %fusion.75, f32[1024]{0:T(1024)S(1)} %dynamic_slice.59, bf16[2048,1024]{1,0:T(8,128)(2,1)} %all-gather.11.cloned.1.call-done, f32[2048]{0:T(1024)S(1)} %compare_convert_fusion, bf16[2048,2048]{1,0:T(8,128)(2,1)} %param.21), kind=kOutput, calls=%fused_computation.74 | convolution fusion | flops 8650750976 | bytes 25182208 | tf_op jit(solution)/shard_map/dot_general | solution.py:156
  433.1 10.9 convolution_convert_fusion.1
  444.1 18.0 %convolution_convert_fusion.2 = bf16[2048,2048]{1,0:T(8,128)(2,1)} fusion(bf16[2048,1024]{1,0:T(8,128)(2,1)} %all-gather.11.cloned.1.call-done, f32[2048,1024]{1,0:T(8,128)} %fusion.75, f32[1024]{0:T(1024)S(1)} %dynamic_slice.59), kind=kOutput, calls=%fused_computation.78 | convolution fusion | flops 8615100416 | bytes 20975616 | tf_op jit(solution)/shard_map/dot_general | solution.py:26
  462.2 157.6 %all-reduce.11.cloned.1.call-done = bf16[2048,2048]{1,0:T(8,128)(2,1)} async-done(((bf16[2048,2048]{1,0:T(8,128)(2,1)}), bf16[2048,2048]{1,0:T(8,128)(2,1)}) %all-reduce.11.cloned.1.call-update) | async-done | bytes 8388624 | tf_op jit(solution)/shard_map/psum | solution.py:161
  619.8 10.3 multiply_reduce_fusion.3
  630.4 21.3 %convert_multiply_fusion = (f32[2048,2048]{1,0:T(8,128)}, f32[2048,2048]{1,0:T(8,128)}) fusion(bf16[2048,2048]{1,0:T(8,128)(2,1)} %param.21, f32[2048]{0:T(1024)S(1)} %compare_convert_fusion, f32[2048]{0:T(1024)S(1)} %broadcast_multiply_fusion, f32[2048]{0:T(1024)S(1)} %broadcast_multiply_fusion.1, f32[2048]{0:T(1024)S(1)} %copy-done.23, ...), kind=kLoop, calls=%fused_computation.59 | loop fusion | flops 46137344 | bytes 67158016 | tf_op jit(solution)/shard_map/mul | solution.py:152
  651.7 9.3 fusion.67
  661.0 89.7 %while.29 = (s32[]{:T(128)}, f32[2048,2,128]{0,2,1:T(8,128)S(1)}, f32[2048,2,128]{0,2,1:T(8,128)}, bf16[4,512,2,128]{3,1,0,2:T(8,128)(2,1)}, s32[4]{0:T(128)S(1)...) while((s32[]{:T(128)}, f32[2048,2,128]{0,2,1:T(8,128)S(1)}, ...), condition=%wide.region_17.18_spmd.clone, body=%wide.region_15.17_spmd.clone.sunk | while | flops 2721709568 | bytes 97040784 | solution.py:220
  668.7 3.7 fusion.149
  672.4 3.9 multiply_reduce_fusion.6
  676.3 2.6 multiply_convert_fusion.6
  690.1 5.0 fusion.149
  695.1 3.9 multiply_reduce_fusion.6
  698.9 2.6 multiply_convert_fusion.6
  702.9 2.4 fusion.148
  712.8 5.0 fusion.149
  717.8 3.8 multiply_reduce_fusion.6
  721.6 2.6 multiply_convert_fusion.6
  735.5 5.0 fusion.149
  740.5 3.9 multiply_reduce_fusion.6
  744.3 2.6 multiply_convert_fusion.6
  752.1 2.5 copy.79
  756.9 2.9 copy.80
  759.8 11.6 convolution_convert_fusion
  772.6 10.0 fusion.70
  782.7 16.9 %fusion.61 = bf16[2048,1024]{1,0:T(8,128)(2,1)} fusion(bf16[2048,2048]{1,0:T(8,128)(2,1)} %param.21, f32[2048]{0:T(1024)S(1)} %copy-done.20, f32[2048,1024]{1,0:T(8,128)} %fusion.75, f32[1024]{0:T(1024)S(1)} %copy-done.31), kind=kOutput, calls=%fused_computation.91 | convolution fusion | flops 8625586176 | bytes 20983808 | tf_op jit(solution)/shard_map/dot_general | solution.py:26
  799.8 15.7 %convolution_convert_fusion.4 = bf16[2048,1024]{1,0:T(8,128)(2,1)} fusion(bf16[2048,1024]{1,0:T(8,128)(2,1)} %copy-done.37, f32[2048,2048]{1,0:T(8,128)} %subtract_multiply_fusion, f32[2048]{0:T(1024)S(1)} %copy-done.34, f32[2048]{0:T(1024)S(1)} %copy-done.24), kind=kOutput, calls=%fused_computation.92 | convolution fusion | flops 8604614656 | bytes 25182208 | tf_op jit(solution)/shard_map/dot_general | solution.py:26
  815.7 11.9 convolution_convert_fusion.5
  828.3 11.4 convert_element_type.149
  842.0 3.3 dynamic-slice_reduce_fusion.1
  845.3 259.9 %all-reduce.17.cloned.1.call-done = (bf16[2048,2048]{1,0:T(8,128)(2,1)}, bf16[2048,2048]{1,0:T(8,128)(2,1)}) async-done(((bf16[2048,2048]{1,0:T(8,128)(2,1)}, bf16[2048,2048]{1,0:T(8,128)(2,1)}), (bf16[2048,2048]{1,0:T(8,128)(2,1)}, bf16[2048,2048]{1,0:T(8,128)(2,1)})) %all-reduce.17.cloned.1.call-update) | async-done | bytes 16777232 | tf_op jit(solution)/shard_map/psum | solution.py:143
  1105.2 3.2 fusion.79
  1108.5 5.2 dynamic-slice_reduce_fusion.2
  1113.8 22.7 %reduce-scatter.7.cloned.1.call-done = bf16[512,256]{1,0:T(8,128)(2,1)} async-done(((bf16[2048,256]{1,0:T(8,128)(2,1)}), bf16[512,256]{1,0:T(8,128)(2,1)}) %reduce-scatter.7.cloned.1.call-update) | async-done | bytes 262160 | tf_op jit(solution)/shard_map/reduce_scatter | solution.py:264
  1138.4 54.2 %reduce-scatter.11.cloned.1.call-done = bf16[512,1024]{1,0:T(8,128)(2,1)} async-done(((bf16[2048,1024]{1,0:T(8,128)(2,1)}), bf16[512,1024]{1,0:T(8,128)(2,1)}) %reduce-scatter.11.cloned.1.call-update) | async-done | bytes 1048592 | tf_op jit(solution)/shard_map/reduce_scatter | solution.py:270
  1192.6 2.8 convert_element_type.165
  1195.4 52.7 %reduce-scatter.9.cloned.1.call-done = bf16[512,1024]{1,0:T(8,128)(2,1)} async-done(((bf16[2048,1024]{1,0:T(8,128)(2,1)}), bf16[512,1024]{1,0:T(8,128)(2,1)}) %reduce-scatter.9.cloned.1.call-update) | async-done | bytes 1048592 | tf_op jit(solution)/shard_map/reduce_scatter | solution.py:267
  1248.1 2.8 convert_element_type.162
  1250.9 44.5 %reduce-scatter.5.cloned.1.call-done = bf16[512,768]{1,0:T(8,128)(2,1)} async-done(((bf16[2048,768]{1,0:T(8,128)(2,1)}), bf16[512,768]{1,0:T(8,128)(2,1)}) %reduce-scatter.5.cloned.1.call-update) | async-done | bytes 786448 | tf_op jit(solution)/shard_map/reduce_scatter | solution.py:261
  1297.7 55.9 %all-reduce.13.cloned.1.call-done = (f32[4096]{0:T(1024)}, f32[2048]{0:T(1024)}, f32[8192]{0:T(1024)}, f32[2048]{0:T(1024)}, f32[2048]{0:T(1024)}, /*index=5*/f32[2048]{0:T(1024)}, f32[2048]{0:T(1024)}, f32[2048]{0:T(1024)}) async-done(((f32[4096]{0:T(1024)}, f32[2048]{0:T(1024)}, f32[8192]{0:T(1024)}, f32[2048]{0:T(1024)}, f32[2048]{0:T(1024)}, /*index=5*/f32[2048]{0:T(1024)}, f32[2048]{0:T(1024)}, ...) | async-done | bytes 98320 | tf_op jit(solution)/shard_map/psum | solution.py:275
  1353.7 3.2 multiply_convert_fusion.2
  1356.8 44.1 %all-reduce.15.cloned.1.call-done = (f32[4096]{0:T(1024)}, f32[2048]{0:T(1024)}, f32[8192]{0:T(1024)}, f32[2048]{0:T(1024)}, f32[2048]{0:T(1024)}, /*index=5*/f32[2048]{0:T(1024)}, f32[2048]{0:T(1024)}, f32[2048]{0:T(1024)}) async-done(((f32[4096]{0:T(1024)}, f32[2048]{0:T(1024)}, f32[8192]{0:T(1024)}, f32[2048]{0:T(1024)}, f32[2048]{0:T(1024)}, /*index=5*/f32[2048]{0:T(1024)}, f32[2048]{0:T(1024)}, ...) | async-done | bytes 98320 | tf_op jit(solution)/shard_map/psum | solution.py:274
  (240 shorter events, 93.6 us)
Async XLA Ops:
  7.2 48.4 %all-gather.5.cloned.1.call-start = ((), (), s32[]{:S(2)}) async-start(), calls=%async_computation.4 | async-start | bytes 3932160 | tf_op jit(solution)/shard_map/all_gather | solution.py:54
  9.6 107.9 %all-gather.7.cloned.1.call-start = ((), (), s32[]{:S(2)}) async-start(), calls=%async_computation.5 | async-start | bytes 1310720 | tf_op jit(solution)/shard_map/all_gather | solution.py:55
  11.5 290.1 %all-reduce.9.cloned.1.call-start = ((), (), s32[]{:S(2)}) async-start(), calls=%async_computation.6 | async-start | bytes 16777216 | tf_op jit(solution)/shard_map/psum | solution.py:131
  13.3 6.0 copy-start.3
  13.4 42.2 %copy-start.25 = (f32[2048]{0:T(1024)S(1)}, f32[2048]{0:T(1024)}, u32[]{:S(2)}) copy-start(f32[2048]{0:T(1024)} %param.32) | copy-start | bytes 24580
  13.4 42.2 %copy-start.35 = (f32[2048]{0:T(1024)S(1)}, f32[2048]{0:T(1024)}, u32[]{:S(2)}) copy-start(f32[2048]{0:T(1024)} %param.33) | copy-start | bytes 24580
  19.2 282.3 %copy-start.16 = (f32[2048]{0:T(1024)}, f32[2048]{0:T(1024)S(1)}, u32[]{:S(2)}) copy-start(f32[2048]{0:T(1024)S(1)} %broadcast_multiply_fusion.3) | copy-start | bytes 24580
  21.6 280.0 %copy-start.21 = (f32[2048]{0:T(1024)}, f32[2048]{0:T(1024)S(1)}, u32[]{:S(2)}) copy-start(f32[2048]{0:T(1024)S(1)} %add_rsqrt_fusion.1) | copy-start | bytes 24580
  117.5 8.3 copy-start
  117.5 8.3 copy-start.4
  117.5 8.3 copy-start.6
  117.5 8.3 copy-start.11
  125.8 175.8 %copy-start.28 = (f32[2048]{0:T(1024)S(1)}, f32[2048]{0:T(1024)}, u32[]{:S(2)}) copy-start(f32[2048]{0:T(1024)} %param.27) | copy-start | bytes 24580
  125.8 230.8 %all-gather.9.cloned.1.call-start = ((), (), s32[]{:S(2)}) async-start(), calls=%async_computation.7 | async-start | bytes 5242880 | tf_op jit(solution)/shard_map/all_gather | solution.py:56
  128.6 283.0 %all-gather.11.cloned.1.call-start = ((), (), s32[]{:S(2)}) async-start(), calls=%async_computation.8 | async-start | bytes 5242880 | tf_op jit(solution)/shard_map/all_gather | solution.py:57
  131.4 488.3 %all-reduce.11.cloned.1.call-start = ((), (), s32[]{:S(2)}) async-start(), calls=%async_computation.9 | async-start | bytes 16777216 | tf_op jit(solution)/shard_map/psum | solution.py:161
  131.5 498.6 %copy-start.19 = (f32[2048]{0:T(1024)}, f32[2048]{0:T(1024)S(1)}, u32[]{:S(2)}) copy-start(f32[2048]{0:T(1024)S(1)} %compare_convert_fusion) | copy-start | bytes 24580
  132.2 311.9 %copy-start.30 = (f32[1024]{0:T(1024)}, f32[1024]{0:T(1024)S(1)}, u32[]{:S(2)}) copy-start(f32[1024]{0:T(1024)S(1)} %dynamic_slice.59) | copy-start | bytes 12292
  326.7 30.0 %copy-start.23 = (f32[2048]{0:T(1024)S(1)}, f32[2048]{0:T(1024)}, u32[]{:S(2)}) copy-start(f32[2048]{0:T(1024)} %param.34) | copy-start | bytes 24580
  326.7 30.0 %copy-start.33 = (f32[2048]{0:T(1024)S(1)}, f32[2048]{0:T(1024)}, u32[]{:S(2)}) copy-start(f32[2048]{0:T(1024)} %param.35) | copy-start | bytes 24580
  411.7 21.5 %copy-start.32 = (bf16[2048,1024]{1,0:T(8,128)(2,1)S(1)}, bf16[2048,1024]{1,0:T(8,128)(2,1)}, u32[]{:S(2)}) copy-start(bf16[2048,1024]{1,0:T(8,128)(2,1)} %all-gather.9.cloned.1.call-done) | copy-start | bytes 12582916
  431.2 1.9 copy-start.37
  444.1 661.2 %all-reduce.17.cloned.1.call-start = ((), (), s32[]{:S(2)}) async-start(), calls=%async_computation.16 | async-start | bytes 33554432 | tf_op jit(solution)/shard_map/psum | solution.py:143
  619.8 10.6 copy-start.2
  630.4 21.3 %copy-start.9 = (bf16[2048,256]{1,0:T(8,128)(2,1)S(1)}, bf16[2048,256]{1,0:T(8,128)(2,1)}, u32[]{:S(2)}) copy-start(bf16[2048,256]{1,0:T(8,128)(2,1)} %all-gather.7.cloned.1.call-done) | copy-start | bytes 3145732
  651.6 9.4 copy-start.1
  651.6 9.4 copy-start.12
  664.4 4.3 copy-start.7
  668.6 3.7 copy-start.5
  676.2 2.6 copy-start.13
  680.2 2.4 copy-start.14
  685.8 4.3 copy-start.7
  690.1 5.0 copy-start.5
  698.9 2.6 copy-start.13
  702.9 2.4 copy-start.14
  708.5 4.3 copy-start.7
  712.8 5.0 copy-start.5
  721.6 2.6 copy-start.13
  725.5 2.4 copy-start.14
  731.2 4.3 copy-start.7
  735.4 5.0 copy-start.5
  744.3 2.6 copy-start.13
  748.3 2.4 copy-start.14
  771.4 1.2 copy-start.8
  771.4 11.3 copy-start.20
  771.4 11.3 copy-start.31
  771.4 365.1 %reduce-scatter.7.cloned.1.call-start = ((), (), s32[]{:S(2)}) async-start(), calls=%async_computation.11 | async-start | bytes 1310720 | tf_op jit(solution)/shard_map/reduce_scatter | solution.py:264
  782.6 17.2 %copy-start.24 = (f32[2048]{0:T(1024)S(1)}, f32[2048]{0:T(1024)}, u32[]{:S(2)}) copy-start(f32[2048]{0:T(1024)} %param.34) | copy-start | bytes 24580
  782.6 17.2 %copy-start.34 = (f32[2048]{0:T(1024)S(1)}, f32[2048]{0:T(1024)}, u32[]{:S(2)}) copy-start(f32[2048]{0:T(1024)} %param.35) | copy-start | bytes 24580
  782.6 409.9 %reduce-scatter.11.cloned.1.call-start = ((), (), s32[]{:S(2)}) async-start(), calls=%async_computation.13 | async-start | bytes 5242880 | tf_op jit(solution)/shard_map/reduce_scatter | solution.py:270
  799.7 15.9 %copy-start.10 = (bf16[2048,2,3,128]{0,3,2,1:T(8,128)(2,1)S(1)}, bf16[2048,2,3,128]{0,3,2,1:T(8,128)(2,1)}, u32[]{:S(2)}) copy-start(bf16[2048,2,3,128]{0,3,2,1:T(8,128)(2,1)} %copy.80) | copy-start | bytes 9437188
  799.7 15.9 %copy-start.17 = (f32[2048]{0:T(1024)S(1)}, f32[2048]{0:T(1024)}, u32[]{:S(2)}) copy-start(f32[2048]{0:T(1024)} %copy-done.16) | copy-start | bytes 24580
  799.7 15.9 %copy-start.22 = (f32[2048]{0:T(1024)S(1)}, f32[2048]{0:T(1024)}, u32[]{:S(2)}) copy-start(f32[2048]{0:T(1024)} %copy-done.21) | copy-start | bytes 24580
  799.7 15.9 %copy-start.26 = (f32[2048]{0:T(1024)S(1)}, f32[2048]{0:T(1024)}, u32[]{:S(2)}) copy-start(f32[2048]{0:T(1024)} %param.32) | copy-start | bytes 24580
  799.7 15.9 %copy-start.36 = (f32[2048]{0:T(1024)S(1)}, f32[2048]{0:T(1024)}, u32[]{:S(2)}) copy-start(f32[2048]{0:T(1024)} %param.33) | copy-start | bytes 24580
  799.7 448.4 %reduce-scatter.9.cloned.1.call-start = ((), (), s32[]{:S(2)}) async-start(), calls=%async_computation.12 | async-start | bytes 5242880 | tf_op jit(solution)/shard_map/reduce_scatter | solution.py:267
  815.5 12.1 copy-start.29
  815.6 479.8 %reduce-scatter.5.cloned.1.call-start = ((), (), s32[]{:S(2)}) async-start(), calls=%async_computation.10 | async-start | bytes 3932160 | tf_op jit(solution)/shard_map/reduce_scatter | solution.py:261
  827.5 526.1 %all-reduce.13.cloned.1.call-start = ((), (), s32[]{:S(2)}) async-start(), calls=%async_computation.14 | async-start | bytes 196608 | tf_op jit(solution)/shard_map/psum | solution.py:275
  828.2 11.4 copy-start.15
  845.3 268.4 %copy-start.18 = (f32[16,2,128]{2,1,0:T(2,128)}, f32[16,2,128]{2,1,0:T(2,128)S(1)}, u32[]{:S(2)}) copy-start(f32[16,2,128]{2,1,0:T(2,128)S(1)} %constant_dynamic-update-slice_fusion) | copy-start | bytes 49156
  1108.5 245.2 %copy-start.27 = (f32[2048]{0:T(1024)S(1)}, f32[2048]{0:T(1024)}, u32[]{:S(2)}) copy-start(f32[2048]{0:T(1024)} %param.31) | copy-start | bytes 24580
  1113.7 287.2 %all-reduce.15.cloned.1.call-start = ((), (), s32[]{:S(2)}) async-start(), calls=%async_computation.15 | async-start | bytes 196608 | tf_op jit(solution)/shard_map/psum | solution.py:274
Sparse Core Ops, SparseCore 0:
  10.4 45.1 all-gather.4
  58.0 26.6 all-gather.6
  125.9 175.5 all-reduce.8
  303.8 52.8 all-gather.8
  358.9 52.6 all-gather.10
  444.2 175.5 all-reduce.10
  771.5 333.6 all-reduce.16
  1108.7 27.8 reduce-scatter.6
  1139.8 52.6 reduce-scatter.10
  1195.4 52.6 reduce-scatter.8
  1251.4 43.9 reduce-scatter.4
  1299.5 54.0 all-reduce.12
  1357.1 43.7 all-reduce.14
